TPU v7x, 32 devices: a whole 2x2x4 slice. The times are simulated.
32 devices in a mesh: gx: 4 (over x, core), gy: 8 (over z, y).
Axes of the slice: x: 2, y: 2, z: 4, core: 2. Of those that a mesh axis runs over, the one named last changes fastest.
Arguments:
- state_field: float32 [128, 128, 16, 256], P('gx', 'gy'), may hold values from -80 to 80
- start_basis: float32 [256, 32], replicated, may hold values from -6 to 6
Outputs:
- core_tensor: float32 [128, 128, 512], P('gx', 'gy')
- z_factor: float32 [256, 32], replicated
- x_triangle: float32 [128, 128], replicated
All inputs are finite; a program needn't handle non-finite values.
Results may differ from a plain program's by a relative error of at most 0.0003.
Values sent between devices are 32-bit elements; how exact they have to be, the bound alone decides.
No kernel may reach another device: no remote copies, remote signals or barrier semaphores. Data moves between devices by JAX's collectives and lax.ppermute only.
A program may use at most 64 MiB of HBM per device.

v0:
```python
import jax
import jax.numpy as jnp
from jax import lax
from jax.sharding import PartitionSpec as P

ITERS = 3
precise = lax.Precision.HIGHEST


def orthonormal(image):
    for repeat in range(2):
        inner_gram = jnp.dot(image.T, image, precision=precise, preferred_element_type=jnp.float32)
        lower_factor = jnp.linalg.cholesky(inner_gram)
        image = lax.linalg.triangular_solve(
            lower_factor, image, left_side=False, lower=True, transpose_a=True
        )
    return image


def local(state_field, start_basis):
    x_cells, y_cells, species, z_cells = state_field.shape
    unfolded = state_field.reshape(x_cells * y_cells * species, z_cells)
    local_gram = lax.dot_general(
        unfolded,
        unfolded,
        (((0,), (0,)), ((), ())),
        precision=precise,
        preferred_element_type=jnp.float32,
    )
    z_basis = start_basis
    gram_z = lax.psum(local_gram, ("gx", "gy"))
    for iteration in range(ITERS):
        z_basis = orthonormal(
            jnp.dot(gram_z, z_basis, precision=precise, preferred_element_type=jnp.float32)
        )
    rank_kept = z_basis.shape[1]
    core_rows = jnp.dot(unfolded, z_basis, precision=precise, preferred_element_type=jnp.float32)
    core_tensor = core_rows.reshape(x_cells, y_cells, species * rank_kept)
    own_rows = core_tensor.reshape(x_cells, -1)
    row_piece = lax.all_gather(core_tensor, "gx", axis=0, tiled=True)
    piece_rows = row_piece.reshape(row_piece.shape[0], -1)
    product = jnp.dot(own_rows, piece_rows.T, precision=precise, preferred_element_type=jnp.float32)
    summed_row = lax.psum(product, "gy")
    gram_x = lax.all_gather(summed_row, "gx", axis=0, tiled=True)
    column_count = y_cells * lax.axis_size("gy") * species * rank_kept
    x_triangle = jnp.linalg.cholesky(gram_x).T / jnp.sqrt(jnp.float32(column_count))
    return (core_tensor, z_basis, x_triangle)


def solution(mesh):
    return jax.shard_map(
        local,
        mesh=mesh,
        in_specs=(P("gx", "gy", None, None), P()),
        out_specs=(P("gx", "gy", None), P(), P()),
        check_vma=False,
    )
```

profile of v0, /device:TPU:0, one launch (start us, length us, event | category | flops | bytes accessed | tf_op | source)
XLA Modules:
  0.0 325.5 jit_solution(4373195180380664984)
XLA Ops:
  7.2 0.0 all-reduce.2.cloned.1.call-start
  7.2 17.8 %convolution_bitcast_fusion.1 = f32[256,256]{1,0:T(8,128)} fusion(f32[32,16,16,256]{3,2,1,0:T(8,128)} %param.5), kind=kOutput, calls=%fused_computation.1 | convolution fusion | flops 6442450944 | bytes 8650752 | tf_op jit(solution)/shard_map/dot_general | solution.py:23
  25.0 0.2 all-gather.2.cloned.1.call-start
  25.3 129.2 %all-reduce.2.cloned.1.call-done = f32[256,256]{1,0:T(8,128)} async-done(((f32[256,256]{1,0:T(8,128)}), f32[256,256]{1,0:T(8,128)}) %all-reduce.2.cloned.1.call-update) | async-done | bytes 262160 | tf_op jit(solution)/shard_map/psum | solution.py:31
  154.5 1.3 fusion.29
  155.8 0.2 fusion.30
  156.0 0.1 copy.29
  156.1 2.9 cholesky.142
  159.0 0.6 compare_reduce_fusion.5
  159.7 0.7 fusion.1
  160.3 2.4 custom-call.13
  162.7 0.2 convolution_bitcast_fusion.7
  163.0 0.2 fusion.31
  163.2 0.1 copy.30
  163.2 2.9 cholesky.153
  166.2 0.6 compare_reduce_fusion.4
  166.8 0.7 fusion.2
  167.5 2.4 custom-call.14
  169.9 0.2 convolution_bitcast_fusion.6
  170.2 1.3 fusion.32
  171.5 0.2 fusion.33
  171.7 0.1 copy.31
  171.7 2.9 cholesky.164
  174.7 0.6 compare_reduce_fusion.3
  175.3 0.7 fusion.3
  176.0 2.4 custom-call.15
  178.4 0.2 convolution_bitcast_fusion.5
  178.7 0.2 fusion.34
  178.9 0.1 copy.32
  178.9 2.9 cholesky.175
  181.9 0.6 compare_reduce_fusion.2
  182.5 0.7 fusion.4
  183.2 2.4 custom-call.16
  185.6 0.2 convolution_bitcast_fusion.4
  185.9 1.3 fusion.35
  187.2 0.2 fusion.36
  187.4 0.1 copy.33
  187.4 2.9 cholesky.186
  190.4 0.6 compare_reduce_fusion.1
  191.0 0.7 fusion.5
  191.7 2.4 custom-call.17
  194.1 0.2 convolution_bitcast_fusion.3
  194.4 0.2 fusion.37
  194.5 0.1 copy.34
  194.6 2.9 cholesky.197
  197.6 0.6 compare_reduce_fusion
  198.2 0.7 fusion.6
  198.9 2.4 custom-call.18
  201.3 0.2 convolution_bitcast_fusion.2
  201.6 10.1 %convolution_bitcast_fusion = f32[8192,32]{0,1:T(8,128)S(1)} fusion(f32[256,32]{0,1:T(8,128)S(1)} %convolution_bitcast_fusion.2, f32[8192,256]{1,0:T(8,128)} %bitcast.112), kind=kOutput, calls=%fused_computation | convolution fusion | flops 805306368 | bytes 9469952 | tf_op jit(solution)/shard_map/dot_general | solution.py:37
  211.7 2.7 copy.35
  214.3 4.4 %reshape.33 = f32[32,16,512]{2,1,0:T(8,128)} reshape(f32[8192,32]{1,0:T(8,128)} %copy.35) | data formatting | bytes 2097152 | tf_op jit(solution)/shard_map/reshape | solution.py:38
  218.7 0.0 all-gather.2.cloned.1.call-update
  218.8 3.5 %reshape_reshape.3 = f32[32,8192]{1,0:T(8,128)S(1)} reshape(f32[8192,32]{1,0:T(8,128)} %copy.35) | data formatting | bytes 2097152 | tf_op jit(solution)/shard_map/reshape;reshape | solution.py:39
  222.3 30.1 %all-gather.2.cloned.1.call-done = f32[128,16,512]{2,1,0:T(8,128)} async-done(((f32[32,16,512]{2,1,0:T(8,128)}), f32[128,16,512]{2,1,0:T(8,128)}) %all-gather.2.cloned.1.call-update) | async-done | bytes 4194320 | tf_op jit(solution)/shard_map/all_gather | solution.py:40
  252.4 5.6 %copy.40 = f32[16,8,16,512]{3,1,2,0:T(8,128)S(1)} copy(f32[16,8,16,512]{3,2,1,0:T(8,128)} %bitcast.113) | data formatting | bytes 8388608
  258.0 4.1 %fusion.38 = f32[32,128]{1,0:T(8,128)S(1)} fusion(f32[32,8192]{1,0:T(8,128)S(1)} %reshape_reshape.3, f32[128,8192]{1,0:T(8,128)S(1)} %bitcast.111), kind=kOutput, calls=%fused_computation.73 | convolution fusion | flops 402653184 | bytes 5259264 | tf_op jit(solution)/shard_map/dot_general | solution.py:42
  262.2 37.1 %psum.15 = f32[32,128]{1,0:T(8,128)S(1)} all-reduce(f32[32,128]{1,0:T(8,128)S(1)} %fusion.38), channel_id=1, replica_groups=mesh['gx'=4,'gy'=8] {'gy'}, use_global_device_ids=true, to_apply=%region_3.6 | all-reduce | flops 4096 | bytes 32768 | tf_op jit(solution)/shard_map/psum | solution.py:43
  299.2 5.5 %all_gather.7 = f32[128,128]{1,0:T(8,128)S(1)} all-gather(f32[32,128]{1,0:T(8,128)S(1)} %psum.15), channel_id=1, replica_groups=mesh['gx'=4,'gy'=8] {'gx'}, dimensions={0}, use_global_device_ids=true | all-gather | bytes 81920 | tf_op jit(solution)/shard_map/all_gather | solution.py:44
  304.7 0.1 copy.37
  304.8 11.7 %cholesky.45 = f32[128,128]{1,0:T(8,128)S(1)} custom-call(f32[128,128]{1,0:T(8,128)S(1)} %fusion), custom_call_target="Cholesky" | custom-call | tf_op jit(solution)/shard_map/jit(cholesky)/cholesky | solution.py:46
  316.6 0.6 compare_reduce_fusion.6
  317.2 0.7 multiply_bitcast_fusion
  317.9 0.7 copy.38
  (19 shorter events, 0.3 us)
Async XLA Ops:
  7.2 147.3 %copy-start = (f32[256,32]{0,1:T(8,128)S(1)}, f32[256,32]{0,1:T(8,128)}, u32[]{:S(2)}) copy-start(f32[256,32]{0,1:T(8,128)} %param.6) | copy-start | bytes 98308
  7.2 147.3 %all-reduce.2.cloned.1.call-start = ((), (), s32[]{:S(2)}) async-start(), calls=%async_computation | async-start | bytes 524288 | tf_op jit(solution)/shard_map/psum | solution.py:31
  25.0 227.4 %all-gather.2.cloned.1.call-start = ((), (), s32[]{:S(2)}) async-start(), calls=%async_computation.1 | async-start | bytes 5242880 | tf_op jit(solution)/shard_map/all_gather | solution.py:40
  201.6 17.2 %copy-start.1 = (f32[256,32]{0,1:T(8,128)}, f32[256,32]{0,1:T(8,128)S(1)}, u32[]{:S(2)}) copy-start(f32[256,32]{0,1:T(8,128)S(1)} %convolution_bitcast_fusion.2) | copy-start | bytes 98308
Sparse Core Ops, SparseCore 0:
  25.2 129.2 all-reduce.1
  218.9 33.4 all-gather.1
where the time goes:
time: 326 us; the launch traced here: 325 us
  waiting for transfers between devices  159 us (49%)
  other arithmetic  53.2 us (16%)
  blocking collectives  42.6 us (13%)
  matrix products  38.3 us (12%)
  local copies, waits for them, and re-layouts  17.4 us (5%)
  between operations  14.3 us (4%)
    psum x1, waiting for transfers between devices, local(): gram_z = lax.psum(local_gram, ('gx', 'gy'))  129 us
    psum x1, blocking collectives, local(): summed_row = lax.psum(product, 'gy')  37.1 us
    all_gather x1, waiting for transfers between devices, local(): row_piece = lax.all_gather(core_tensor, 'gx', axis=0, tiled=True)  30.1 us
    another operation x18, other arithmetic, orthonormal(): lower_factor = jnp.linalg.cholesky(inner_gram)  21.6 us
    another operation x12, other arithmetic, orthonormal(): lax.linalg.triangular_solve(lower_factor, image, left_side=False, lower=T...  18.5 us
    dot_general x1, matrix products, local(): lax.dot_general(unfolded, unfolded, (((0,), (0,)), ((), ())), precision=p...  17.8 us
    another operation x3, other arithmetic, local(): jnp.linalg.cholesky(gram_x).T / jnp.sqrt(jnp.float32(column_count))  12.4 us
    dot_general x1, matrix products, local(): jnp.dot(unfolded, z_basis, precision=precise, preferred_element_type=jnp....  10.1 us
  transfers between devices with their start and end apart: 2, of which 2 were waited for; matrix products, arithmetic and copies ran while one was open for 1% of the time, Pallas kernels for 0%

commit v1 on v0

--- a/solution.py
+++ b/solution.py
@@ -28,7 +28,9 @@
         preferred_element_type=jnp.float32,
     )
     z_basis = start_basis
-    gram_z = lax.psum(local_gram, ("gx", "gy"))
+    gram_z = local_gram
+    for axis in ("gy", "gx"):
+        gram_z = lax.psum(gram_z, axis)
     for iteration in range(ITERS):
         z_basis = orthonormal(
             jnp.dot(gram_z, z_basis, precision=precise, preferred_element_type=jnp.float32)

time: 326 us -> 305 us (0.936)
  waiting for transfers between devices: 159 us -> 139 us
    psum x1 -> x2, waiting for transfers between devices: 129 us -> 107 us  [local(): gram_z = lax.psum(gram_z, axis)]
  transfers between devices with their start and end apart: 2 -> 3, of which waited for: 2 -> 3; matrix products, arithmetic and copies ran while one was open for 1% -> 1% of each run, Pallas kernels for 0% -> 0%
where the time goes in v1:
time: 305 us; the launch traced here: 304 us
  waiting for transfers between devices  139 us (46%)
  other arithmetic  53.2 us (17%)
  blocking collectives  42.6 us (14%)
  matrix products  38.3 us (13%)
  local copies, waits for them, and re-layouts  17.4 us (6%)
  between operations  14 us (5%)
    psum x2, waiting for transfers between devices, local(): gram_z = lax.psum(gram_z, axis)  107 us
    psum x1, blocking collectives, local(): summed_row = lax.psum(product, 'gy')  37.1 us
    all_gather x1, waiting for transfers between devices, local(): row_piece = lax.all_gather(core_tensor, 'gx', axis=0, tiled=True)  31.1 us
    another operation x18, other arithmetic, orthonormal(): lower_factor = jnp.linalg.cholesky(inner_gram)  21.6 us
    another operation x12, other arithmetic, orthonormal(): lax.linalg.triangular_solve(lower_factor, image, left_side=False, lower=T...  18.5 us
    dot_general x1, matrix products, local(): lax.dot_general(unfolded, unfolded, (((0,), (0,)), ((), ())), precision=p...  17.8 us
    another operation x3, other arithmetic, local(): jnp.linalg.cholesky(gram_x).T / jnp.sqrt(jnp.float32(column_count))  12.4 us
    dot_general x1, matrix products, local(): jnp.dot(unfolded, z_basis, precision=precise, preferred_element_type=jnp....  10.1 us
  transfers between devices with their start and end apart: 3, of which 3 were waited for; matrix products, arithmetic and copies ran while one was open for 1% of the time, Pallas kernels for 0%

profile of v1, /device:TPU:0, one launch (start us, length us, event | category | flops | bytes accessed | tf_op | source)
XLA Modules:
  0.0 304.3 jit_solution(13083884283183938267)
XLA Ops:
  7.2 17.8 %convolution_bitcast_fusion.1 = f32[256,256]{1,0:T(8,128)} fusion(f32[32,16,16,256]{3,2,1,0:T(8,128)} %param.5), kind=kOutput, calls=%fused_computation.1 | convolution fusion | flops 6442450944 | bytes 8650752 | tf_op jit(solution)/shard_map/dot_general | solution.py:23
  25.0 0.0 all-reduce.5.cloned.1.call-start
  25.1 73.8 %all-reduce.3.cloned.1.call-done = f32[256,256]{1,0:T(8,128)} async-done(((f32[256,256]{1,0:T(8,128)}), f32[256,256]{1,0:T(8,128)}) %all-reduce.3.cloned.1.call-update) | async-done | bytes 262160 | tf_op jit(solution)/shard_map/psum | solution.py:33
  98.9 0.2 all-gather.2.cloned.1.call-start
  99.2 33.6 %all-reduce.5.cloned.1.call-done = f32[256,256]{1,0:T(8,128)} async-done(((f32[256,256]{1,0:T(8,128)}), f32[256,256]{1,0:T(8,128)}) %all-reduce.5.cloned.1.call-update) | async-done | bytes 262160 | tf_op jit(solution)/shard_map/psum | solution.py:33
  132.8 1.3 fusion.29
  134.1 0.2 fusion.30
  134.2 0.1 copy.29
  134.3 2.9 cholesky.142
  137.3 0.6 compare_reduce_fusion.5
  137.9 0.7 fusion.1
  138.6 2.4 custom-call.13
  141.0 0.2 convolution_bitcast_fusion.7
  141.3 0.2 fusion.31
  141.4 0.1 copy.30
  141.5 2.9 cholesky.153
  144.5 0.6 compare_reduce_fusion.4
  145.1 0.7 fusion.2
  145.8 2.4 custom-call.14
  148.2 0.2 convolution_bitcast_fusion.6
  148.4 1.3 fusion.32
  149.7 0.2 fusion.33
  149.9 0.1 copy.31
  150.0 2.9 cholesky.164
  152.9 0.6 compare_reduce_fusion.3
  153.6 0.7 fusion.3
  154.3 2.4 custom-call.15
  156.7 0.2 convolution_bitcast_fusion.5
  156.9 0.2 fusion.34
  157.1 0.1 copy.32
  157.2 2.9 cholesky.175
  160.1 0.6 compare_reduce_fusion.2
  160.8 0.7 fusion.4
  161.4 2.4 custom-call.16
  163.9 0.2 convolution_bitcast_fusion.4
  164.1 1.3 fusion.35
  165.4 0.2 fusion.36
  165.6 0.1 copy.33
  165.7 2.9 cholesky.186
  168.6 0.6 compare_reduce_fusion.1
  169.3 0.7 fusion.5
  169.9 2.4 custom-call.17
  172.4 0.2 convolution_bitcast_fusion.3
  172.6 0.2 fusion.37
  172.8 0.1 copy.34
  172.9 2.9 cholesky.197
  175.8 0.6 compare_reduce_fusion
  176.5 0.7 fusion.6
  177.1 2.4 custom-call.18
  179.6 0.2 convolution_bitcast_fusion.2
  179.8 10.1 %convolution_bitcast_fusion = f32[8192,32]{0,1:T(8,128)S(1)} fusion(f32[256,32]{0,1:T(8,128)S(1)} %convolution_bitcast_fusion.2, f32[8192,256]{1,0:T(8,128)} %bitcast.112), kind=kOutput, calls=%fused_computation | convolution fusion | flops 805306368 | bytes 9469952 | tf_op jit(solution)/shard_map/dot_general | solution.py:39
  189.9 2.7 copy.35
  192.6 4.4 %reshape.33 = f32[32,16,512]{2,1,0:T(8,128)} reshape(f32[8192,32]{1,0:T(8,128)} %copy.35) | data formatting | bytes 2097152 | tf_op jit(solution)/shard_map/reshape | solution.py:40
  197.0 3.5 %reshape_reshape.3 = f32[32,8192]{1,0:T(8,128)S(1)} reshape(f32[8192,32]{1,0:T(8,128)} %copy.35) | data formatting | bytes 2097152 | tf_op jit(solution)/shard_map/reshape;reshape | solution.py:41
  200.5 31.1 %all-gather.2.cloned.1.call-done = f32[128,16,512]{2,1,0:T(8,128)} async-done(((f32[32,16,512]{2,1,0:T(8,128)}), f32[128,16,512]{2,1,0:T(8,128)}) %all-gather.2.cloned.1.call-update) | async-done | bytes 4194320 | tf_op jit(solution)/shard_map/all_gather | solution.py:42
  231.6 5.6 %copy.40 = f32[16,8,16,512]{3,1,2,0:T(8,128)S(1)} copy(f32[16,8,16,512]{3,2,1,0:T(8,128)} %bitcast.113) | data formatting | bytes 8388608
  237.2 4.1 %fusion.38 = f32[32,128]{1,0:T(8,128)S(1)} fusion(f32[32,8192]{1,0:T(8,128)S(1)} %reshape_reshape.3, f32[128,8192]{1,0:T(8,128)S(1)} %bitcast.111), kind=kOutput, calls=%fused_computation.73 | convolution fusion | flops 402653184 | bytes 5259264 | tf_op jit(solution)/shard_map/dot_general | solution.py:44
  241.4 37.1 %psum.23 = f32[32,128]{1,0:T(8,128)S(1)} all-reduce(f32[32,128]{1,0:T(8,128)S(1)} %fusion.38), channel_id=1, replica_groups=mesh['gx'=4,'gy'=8] {'gy'}, use_global_device_ids=true, to_apply=%region_4.7 | all-reduce | flops 4096 | bytes 32768 | tf_op jit(solution)/shard_map/psum | solution.py:45
  278.4 5.5 %all_gather.7 = f32[128,128]{1,0:T(8,128)S(1)} all-gather(f32[32,128]{1,0:T(8,128)S(1)} %psum.23), channel_id=1, replica_groups=mesh['gx'=4,'gy'=8] {'gx'}, dimensions={0}, use_global_device_ids=true | all-gather | bytes 81920 | tf_op jit(solution)/shard_map/all_gather | solution.py:46
  283.9 0.1 copy.37
  284.0 11.7 %cholesky.45 = f32[128,128]{1,0:T(8,128)S(1)} custom-call(f32[128,128]{1,0:T(8,128)S(1)} %fusion), custom_call_target="Cholesky" | custom-call | tf_op jit(solution)/shard_map/jit(cholesky)/cholesky | solution.py:48
  295.8 0.6 compare_reduce_fusion.6
  296.4 0.7 multiply_bitcast_fusion
  297.1 0.7 copy.38
  (22 shorter events, 0.4 us)
Async XLA Ops:
  7.2 125.6 %copy-start = (f32[256,32]{0,1:T(8,128)S(1)}, f32[256,32]{0,1:T(8,128)}, u32[]{:S(2)}) copy-start(f32[256,32]{0,1:T(8,128)} %param.6) | copy-start | bytes 98308
  7.2 91.7 %all-reduce.3.cloned.1.call-start = ((), (), s32[]{:S(2)}) async-start(), calls=%async_computation | async-start | bytes 524288 | tf_op jit(solution)/shard_map/psum | solution.py:33
  25.0 107.7 %all-reduce.5.cloned.1.call-start = ((), (), s32[]{:S(2)}) async-start(), calls=%async_computation.1 | async-start | bytes 524288 | tf_op jit(solution)/shard_map/psum | solution.py:33
  98.9 132.7 %all-gather.2.cloned.1.call-start = ((), (), s32[]{:S(2)}) async-start(), calls=%async_computation.2 | async-start | bytes 5242880 | tf_op jit(solution)/shard_map/all_gather | solution.py:42
  179.8 17.2 %copy-start.1 = (f32[256,32]{0,1:T(8,128)}, f32[256,32]{0,1:T(8,128)S(1)}, u32[]{:S(2)}) copy-start(f32[256,32]{0,1:T(8,128)S(1)} %convolution_bitcast_fusion.2) | copy-start | bytes 98308
Sparse Core Ops, SparseCore 0:
  25.2 73.7 all-reduce.2
  101.2 31.4 all-reduce.4
  197.1 34.4 all-gather.1

commit v2 on v0

--- a/solution.py
+++ b/solution.py
@@ -37,7 +37,10 @@
     core_rows = jnp.dot(unfolded, z_basis, precision=precise, preferred_element_type=jnp.float32)
     core_tensor = core_rows.reshape(x_cells, y_cells, species * rank_kept)
     own_rows = core_tensor.reshape(x_cells, -1)
-    row_piece = lax.all_gather(core_tensor, "gx", axis=0, tiled=True)
+    size = lax.axis_size("gx")
+    blocks = jnp.stack([core_tensor for _ in range(size)])
+    blocks = lax.all_to_all(blocks, "gx", split_axis=0, concat_axis=0)
+    row_piece = jnp.concatenate(blocks, axis=0)
     piece_rows = row_piece.reshape(row_piece.shape[0], -1)
     product = jnp.dot(own_rows, piece_rows.T, precision=precise, preferred_element_type=jnp.float32)
     summed_row = lax.psum(product, "gy")

time: 326 us -> 346 us (1.061)
  waiting for transfers between devices: 159 us -> 174 us
  starting transfers between devices: 0.26 us -> 4.9 us
    all_to_all x0 -> x1, waiting for transfers between devices: none -> 44.7 us  [local(): blocks = lax.all_to_all(blocks, 'gx', split_axis=0, concat_axis=0)]
    all_gather x1 -> x0, waiting for transfers between devices: 30.1 us -> none  [local(): row_piece = lax.all_gather(core_tensor, 'gx', axis=0, tiled=True)]
    all_to_all x0 -> x1, starting transfers between devices: none -> 4.86 us  [local(): blocks = lax.all_to_all(blocks, 'gx', split_axis=0, concat_axis=0)]
where the time goes in v2:
time: 346 us; the launch traced here: 345 us
  waiting for transfers between devices  174 us (50%)
  other arithmetic  53.2 us (15%)
  blocking collectives  41.3 us (12%)
  matrix products  38.2 us (11%)
  local copies, waits for them, and re-layouts  19.1 us (6%)
  between operations  14.3 us (4%)
  starting transfers between devices  4.9 us (1%)
    psum x1, waiting for transfers between devices, local(): gram_z = lax.psum(local_gram, ('gx', 'gy'))  129 us
    all_to_all x1, waiting for transfers between devices, local(): blocks = lax.all_to_all(blocks, 'gx', split_axis=0, concat_axis=0)  44.7 us
    psum x1, blocking collectives, local(): summed_row = lax.psum(product, 'gy')  36.1 us
    another operation x18, other arithmetic, orthonormal(): lower_factor = jnp.linalg.cholesky(inner_gram)  21.6 us
    another operation x12, other arithmetic, orthonormal(): lax.linalg.triangular_solve(lower_factor, image, left_side=False, lower=T...  18.5 us
    dot_general x1, matrix products, local(): lax.dot_general(unfolded, unfolded, (((0,), (0,)), ((), ())), precision=p...  17.7 us
    another operation x3, other arithmetic, local(): jnp.linalg.cholesky(gram_x).T / jnp.sqrt(jnp.float32(column_count))  12.4 us
    dot_general x1, matrix products, local(): jnp.dot(unfolded, z_basis, precision=precise, preferred_element_type=jnp....  10 us
  transfers between devices with their start and end apart: 2, of which 2 were waited for; matrix products, arithmetic and copies ran while one was open for 1% of the time, Pallas kernels for 0%

profile of v2, /device:TPU:0, one launch (start us, length us, event | category | flops | bytes accessed | tf_op | source)
XLA Modules:
  0.0 345.2 jit_solution(9829408684265592677)
XLA Ops:
  7.2 0.0 all-reduce.2.cloned.1.call-start
  7.2 17.7 %convolution_bitcast_fusion.1 = f32[256,256]{1,0:T(8,128)} fusion(f32[32,16,16,256]{3,2,1,0:T(8,128)} %param.5), kind=kOutput, calls=%fused_computation.1 | convolution fusion | flops 6442450944 | bytes 8650752 | tf_op jit(solution)/shard_map/dot_general | solution.py:23
  24.9 129.5 %all-reduce.2.cloned.1.call-done = f32[256,256]{1,0:T(8,128)} async-done(((f32[256,256]{1,0:T(8,128)}), f32[256,256]{1,0:T(8,128)}) %all-reduce.2.cloned.1.call-update) | async-done | bytes 262160 | tf_op jit(solution)/shard_map/psum | solution.py:31
  154.4 1.3 fusion.29
  155.7 0.2 fusion.30
  155.9 0.1 copy.29
  156.0 2.9 cholesky.142
  158.9 0.6 compare_reduce_fusion.5
  159.6 0.7 fusion.1
  160.2 2.4 custom-call.13
  162.7 0.2 convolution_bitcast_fusion.7
  162.9 0.2 fusion.31
  163.1 0.1 copy.30
  163.2 2.9 cholesky.153
  166.1 0.6 compare_reduce_fusion.4
  166.8 0.7 fusion.2
  167.4 2.4 custom-call.14
  169.9 0.2 convolution_bitcast_fusion.6
  170.1 1.3 fusion.32
  171.4 0.2 fusion.33
  171.6 0.1 copy.31
  171.7 2.9 cholesky.164
  174.6 0.6 compare_reduce_fusion.3
  175.3 0.7 fusion.3
  175.9 2.4 custom-call.15
  178.4 0.2 convolution_bitcast_fusion.5
  178.6 0.2 fusion.34
  178.8 0.1 copy.32
  178.9 2.9 cholesky.175
  181.8 0.6 compare_reduce_fusion.2
  182.5 0.7 fusion.4
  183.1 2.4 custom-call.16
  185.6 0.2 convolution_bitcast_fusion.4
  185.8 1.3 fusion.35
  187.1 0.2 fusion.36
  187.3 0.1 copy.33
  187.4 2.9 cholesky.186
  190.3 0.6 compare_reduce_fusion.1
  191.0 0.7 fusion.5
  191.6 2.4 custom-call.17
  194.1 0.2 convolution_bitcast_fusion.3
  194.3 0.2 fusion.37
  194.5 0.1 copy.34
  194.6 2.9 cholesky.197
  197.5 0.6 compare_reduce_fusion
  198.2 0.7 fusion.6
  198.8 2.4 custom-call.18
  201.3 0.2 convolution_bitcast_fusion.2
  201.5 10.0 %convolution_bitcast_fusion = f32[8192,32]{0,1:T(8,128)S(1)} fusion(f32[256,32]{0,1:T(8,128)S(1)} %convolution_bitcast_fusion.2, f32[8192,256]{1,0:T(8,128)} %bitcast.113), kind=kOutput, calls=%fused_computation | convolution fusion | flops 805306368 | bytes 9469952 | tf_op jit(solution)/shard_map/dot_general | solution.py:37
  211.6 2.7 copy.35
  214.2 3.5 %reshape.32 = f32[32,16,512]{2,1,0:T(8,128)S(1)} reshape(f32[8192,32]{1,0:T(8,128)} %copy.35) | data formatting | bytes 2097152 | tf_op jit(solution)/shard_map/reshape | solution.py:38
  217.8 2.5 stack.3
  220.3 4.9 %all-to-all-start = ((f32[4,32,16,512]{3,2,1,0:T(8,128)}), f32[4,32,16,512]{3,2,1,0:T(8,128)}, u32[]{:S(2)}, u32[]{:S(2)}) async-start(f32[4,32,16,512]{3,2,1,0:T(8,128)} %stack.3), calls=%async_computation | async-start | bytes 8388608 | tf_op jit(solution)/shard_map/all_to_all | solution.py:42
  225.2 3.5 %reshape_reshape.6 = f32[32,8192]{1,0:T(8,128)S(1)} reshape(f32[8192,32]{1,0:T(8,128)} %copy.35) | data formatting | bytes 2097152 | tf_op jit(solution)/shard_map/reshape;reshape | solution.py:39
  228.7 44.7 %all-to-all-done = f32[4,32,16,512]{3,2,1,0:T(8,128)} async-done(((f32[4,32,16,512]{3,2,1,0:T(8,128)}), f32[4,32,16,512]{3,2,1,0:T(8,128)}, u32[]{:S(2)}, u32[]{:S(2)}) %all-to-all-start) | async-done | bytes 4194336 | tf_op jit(solution)/shard_map/all_to_all | solution.py:42
  273.4 5.6 %copy.40 = f32[16,8,16,512]{3,1,2,0:T(8,128)S(1)} copy(f32[16,8,16,512]{3,2,1,0:T(8,128)} %bitcast.32) | data formatting | bytes 8388608
  279.0 4.1 %fusion.38 = f32[32,128]{1,0:T(8,128)S(1)} fusion(f32[32,8192]{1,0:T(8,128)S(1)} %reshape_reshape.6, f32[128,8192]{1,0:T(8,128)S(1)} %bitcast.112), kind=kOutput, calls=%fused_computation.73 | convolution fusion | flops 402653184 | bytes 5259264 | tf_op jit(solution)/shard_map/dot_general | solution.py:45
  283.1 36.1 %psum.15 = f32[32,128]{1,0:T(8,128)S(1)} all-reduce(f32[32,128]{1,0:T(8,128)S(1)} %fusion.38), channel_id=1, replica_groups=mesh['gx'=4,'gy'=8] {'gy'}, use_global_device_ids=true, to_apply=%region_3.6 | all-reduce | flops 4096 | bytes 32768 | tf_op jit(solution)/shard_map/psum | solution.py:46
  319.3 5.2 %all_gather.3 = f32[128,128]{1,0:T(8,128)S(1)} all-gather(f32[32,128]{1,0:T(8,128)S(1)} %psum.15), channel_id=1, replica_groups=mesh['gx'=4,'gy'=8] {'gx'}, dimensions={0}, use_global_device_ids=true | all-gather | bytes 81920 | tf_op jit(solution)/shard_map/all_gather | solution.py:47
  324.5 0.1 copy.37
  324.6 11.7 %cholesky.45 = f32[128,128]{1,0:T(8,128)S(1)} custom-call(f32[128,128]{1,0:T(8,128)S(1)} %fusion), custom_call_target="Cholesky" | custom-call | tf_op jit(solution)/shard_map/jit(cholesky)/cholesky | solution.py:49
  336.3 0.6 compare_reduce_fusion.6
  337.0 0.7 multiply_bitcast_fusion
  337.6 0.7 copy.38
  (21 shorter events, 0.3 us)
Async XLA Ops:
  7.2 147.3 %copy-start = (f32[256,32]{0,1:T(8,128)S(1)}, f32[256,32]{0,1:T(8,128)}, u32[]{:S(2)}) copy-start(f32[256,32]{0,1:T(8,128)} %param.6) | copy-start | bytes 98308
  7.2 147.3 %all-reduce.2.cloned.1.call-start = ((), (), s32[]{:S(2)}) async-start(), calls=%async_computation.1 | async-start | bytes 524288 | tf_op jit(solution)/shard_map/psum | solution.py:31
  201.5 16.3 %copy-start.2 = (f32[256,32]{0,1:T(8,128)}, f32[256,32]{0,1:T(8,128)S(1)}, u32[]{:S(2)}) copy-start(f32[256,32]{0,1:T(8,128)S(1)} %convolution_bitcast_fusion.2) | copy-start | bytes 98308
  217.8 10.9 %copy-start.1 = (f32[32,16,512]{2,1,0:T(8,128)}, f32[32,16,512]{2,1,0:T(8,128)S(1)}, u32[]{:S(2)}) copy-start(f32[32,16,512]{2,1,0:T(8,128)S(1)} %reshape.32) | copy-start | bytes 3145732
  220.3 53.1 %all-to-all-start = ((f32[4,32,16,512]{3,2,1,0:T(8,128)}), f32[4,32,16,512]{3,2,1,0:T(8,128)}, u32[]{:S(2)}, u32[]{:S(2)}) async-start(f32[4,32,16,512]{3,2,1,0:T(8,128)} %stack.3), calls=%async_computation | async-start | bytes 8388608 | tf_op jit(solution)/shard_map/all_to_all | solution.py:42
Sparse Core Ops, SparseCore 0:
  25.1 129.3 all-reduce.1
